TPU v7x, 32 devices: a whole 2x2x4 slice. The times are simulated.
32 devices in a mesh: leaf: 8 (over z, y), rhs: 4 (over x, core).
Axes of the slice: x: 2, y: 2, z: 4, core: 2. Of those that a mesh axis runs over, the one named last changes fastest.
Arguments:
- leaf_parents: int32 [32], replicated, may hold values from 0 to 15, as said below
- mid_parents: int32 [16], replicated, may hold values from 0 to 7, as said below
- leaf_codes: int32 [32, 1], replicated, may hold values from 0 to 7, as said below
- mid_codes: int32 [16, 1], replicated, may hold values from 0 to 3, as said below
- leaf_valid: int32 [32], P('leaf'), may hold values from 1 to 128
- mid_valid: int32 [16], P('leaf'), may hold values from 1 to 128
- leaf_inverse: bfloat16 [32, 512, 512], P('leaf')
- mid_inverse: bfloat16 [16, 512, 512], P('leaf')
- top_inverse: bfloat16 [8, 512, 512], P('leaf')
- leaf_panels: bfloat16 [32, 128, 512], P('leaf'), may hold values from -0.1875 to 0.1875
- mid_panels: bfloat16 [16, 128, 512], P('leaf'), may hold values from -0.1875 to 0.1875
- leaf_cotangent: bfloat16 [32, 128, 512], P('leaf', 'rhs'), may hold values from -6 to 6
- mid_cotangent: bfloat16 [16, 128, 512], P('leaf', 'rhs'), may hold values from -6 to 6
- top_cotangent: bfloat16 [8, 128, 512], P('leaf', 'rhs'), may hold values from -6 to 6
- mid_primal: bfloat16 [16, 128, 512], P('leaf', 'rhs'), may hold values from -0.59765625 to 0.59765625
- top_primal: bfloat16 [8, 128, 512], P('leaf', 'rhs'), may hold values from -0.59765625 to 0.59765625
Outputs:
- leaf_adjoint: bfloat16 [32, 128, 512], P('leaf', 'rhs')
- mid_adjoint: bfloat16 [16, 128, 512], P('leaf', 'rhs')
- top_adjoint: bfloat16 [8, 128, 512], P('leaf', 'rhs')
- leaf_grad: bfloat16 [32, 128, 512], P('leaf', 'rhs')
- mid_grad: bfloat16 [16, 128, 512], P('leaf', 'rhs')
Inputs may be any that keep to these rules, and one draw needn't show every extreme that they name: `leaf_parents`: the parent of level-0 supernode s is level-1 supernode s // 2 or one beside it. `mid_parents`: the parent of level-1 supernode p is level-2 supernode p // 2 or one beside it; it is p // 2 + 1 whenever p % 4 == 3 and p < 15. `leaf_codes`: the 1 codes of one panel are distinct. `mid_codes`: the 1 codes of one panel are distinct.
All inputs are finite; a program needn't handle non-finite values.
Results may differ from a plain program's by a relative error of at most 0.0053.
Values may be sent and summed in bfloat16 or wider, within the bound.
No kernel may reach another device: no remote copies, remote signals or barrier semaphores. Data moves between devices by JAX's collectives and lax.ppermute only.
A program may use at most 64 MiB of HBM per device.

v0:
```python
import jax
import jax.numpy as jnp
from jax import lax
from jax.sharding import PartitionSpec as P

BLK = 128
MR = 128
NB = 4


def padded(block, sides, width):
    for axis, dim in sides:
        count = lax.axis_size(axis)
        forward = [(i, i + 1) for i in range(count - 1)]
        backward = [(target, source) for source, target in forward]
        low = lax.ppermute(
            lax.slice_in_dim(block, block.shape[dim] - width, None, axis=dim), axis, forward
        )
        high = lax.ppermute(lax.slice_in_dim(block, 0, width, axis=dim), axis, backward)
        block = jnp.concatenate([low, block, high], axis=dim)
    return block


def from_behind(value, axis, by):
    peers = lax.axis_size(axis)
    pairs = [(i, i + by) for i in range(peers) if 0 <= i + by < peers]
    return lax.ppermute(value, axis, pairs)


def solve_level(block_rows, inverse):
    return lax.dot_general(
        block_rows, inverse, (((2,), (2,)), ((0,), (0,))), preferred_element_type=jnp.float32
    )


def mask_columns(block_rows, row_limit):
    columns = jnp.arange(block_rows.shape[2], dtype=jnp.int32)
    return jnp.where(
        columns[None, None, :] < row_limit[:, None, None], block_rows, jnp.zeros_like(block_rows)
    )


def panel_update(adjoint_rows, panel_block, row_limit):
    update = lax.dot_general(
        adjoint_rows, panel_block, (((2,), (2,)), ((0,), (0,))), preferred_element_type=jnp.float32
    )
    return mask_columns(update, row_limit)


def tile_grad(rows_block, adjoint_block):
    return -lax.dot_general(
        rows_block, adjoint_block, (((1,), (1,)), ((0,), (0,))), preferred_element_type=jnp.float32
    )


def table_pick(table, wanted):
    entries = table.shape[0]
    match = wanted[:, None] == jnp.arange(entries, dtype=jnp.int32)[None, :]
    extra = table.ndim - 1
    spread_match = match.reshape(match.shape + (1,) * extra)
    values = jnp.sum(jnp.where(spread_match, table[None], 0), axis=1)
    found = jnp.any(match, axis=1).reshape((wanted.shape[0],) + (1,) * extra)
    return jnp.where(found, values, -1)


def route_blocks(extended, targets, code_ids, own_nodes, offset):
    src_count = extended.shape[0]
    probe_count = extended.shape[1]
    code_count = code_ids.shape[1]
    block_width = extended.shape[2] // code_count
    blocks = jnp.arange(NB, dtype=jnp.int32)
    matched = (targets[None, :, None, None] == own_nodes[:, None, None, None]) & (
        code_ids[None, :, :, None] - offset == blocks[None, None, None, :]
    )
    weights = matched.astype(jnp.float32)
    pieces = extended.reshape(src_count, probe_count, code_count, block_width)
    placed = jnp.einsum("temb,enmc->tnbc", weights, pieces, precision=lax.Precision.HIGHEST)
    return placed.reshape(own_nodes.shape[0], probe_count, NB * block_width)


def pick_rows(extended, ext_ids, wanted, code_ids, offset):
    src_count = extended.shape[0]
    probe_count = extended.shape[1]
    blocks = jnp.arange(NB, dtype=jnp.int32)
    matched = (ext_ids[None, None, :, None] == wanted[:, None, None, None]) & (
        code_ids[:, :, None, None] - offset == blocks[None, None, None, :]
    )
    weights = matched.astype(jnp.bfloat16)
    pieces = extended.reshape(src_count, probe_count, NB, BLK)
    chosen = jnp.einsum("smeb,enbc->snmc", weights, pieces, preferred_element_type=jnp.float32)
    return chosen.reshape(wanted.shape[0], probe_count, MR)


def shards(
    leaf_parents,
    mid_parents,
    leaf_codes,
    mid_codes,
    leaf_valid,
    mid_valid,
    leaf_inverse,
    mid_inverse,
    top_inverse,
    leaf_panels,
    mid_panels,
    leaf_cotangent,
    mid_cotangent,
    top_cotangent,
    mid_primal,
    top_primal,
):
    leaf_count = leaf_inverse.shape[0]
    mid_count = mid_inverse.shape[0]
    top_count = top_inverse.shape[0]
    device = lax.axis_index("leaf")
    leaf_first = device * leaf_count
    mid_first = device * mid_count
    top_first = device * top_count
    own_mid_nodes = mid_first + jnp.arange(mid_count, dtype=jnp.int32)
    own_top_nodes = top_first + jnp.arange(top_count, dtype=jnp.int32)
    leaf_near_ids = leaf_first - leaf_count + jnp.arange(3 * leaf_count, dtype=jnp.int32)
    mid_near_ids = mid_first - mid_count + jnp.arange(3 * mid_count, dtype=jnp.int32)
    top_far_ids = top_first - 2 * top_count + jnp.arange(5 * top_count, dtype=jnp.int32)
    own_leaf_parents = lax.dynamic_slice_in_dim(leaf_parents, leaf_first, leaf_count, 0)
    own_leaf_codes = lax.dynamic_slice_in_dim(leaf_codes, leaf_first, leaf_count, 0)
    own_mid_parents = lax.dynamic_slice_in_dim(mid_parents, mid_first, mid_count, 0)
    own_mid_codes = lax.dynamic_slice_in_dim(mid_codes, mid_first, mid_count, 0)
    own_leaf_grand = table_pick(mid_parents, own_leaf_parents)
    near_mid_parents = table_pick(mid_parents, mid_near_ids)
    near_mid_codes = table_pick(mid_codes, mid_near_ids)
    parent_ext = padded(mid_primal, (("leaf", 0),), mid_count)
    grand_moved = [from_behind(top_primal, "leaf", step) for step in (2, 1, -1, -2)]
    grand_ext = jnp.concatenate(
        [grand_moved[0], grand_moved[1], top_primal, grand_moved[2], grand_moved[3]], axis=0
    )
    leaf_adjoint = solve_level(leaf_cotangent, leaf_inverse).astype(jnp.bfloat16)
    leaf_update = panel_update(leaf_adjoint, leaf_panels, leaf_valid)
    nearby = padded(leaf_update, (("leaf", 0),), leaf_count)
    near_parents = table_pick(leaf_parents, leaf_near_ids)
    near_codes = table_pick(leaf_codes, leaf_near_ids)
    to_middle = route_blocks(nearby, near_parents, near_codes, own_mid_nodes, 0)
    carried = route_blocks(nearby, near_parents, near_codes, own_mid_nodes, NB)
    middle_accum = mid_cotangent.astype(jnp.float32) - to_middle
    mid_adjoint = solve_level(middle_accum.astype(jnp.bfloat16), mid_inverse).astype(jnp.bfloat16)
    middle_update = panel_update(mid_adjoint, mid_panels, mid_valid)
    packed = jnp.concatenate([middle_update, carried], axis=2)
    mid_near = padded(packed, (("leaf", 0),), mid_count)
    width_split = middle_update.shape[2]
    to_top = route_blocks(
        mid_near[:, :, :width_split], near_mid_parents, near_mid_codes, own_top_nodes, 0
    )
    owner_hits = (near_mid_parents[None, :] == own_top_nodes[:, None]).astype(jnp.float32)
    to_top = to_top + jnp.einsum(
        "te,enw->tnw", owner_hits, mid_near[:, :, width_split:], precision=lax.Precision.HIGHEST
    )
    top_accum = top_cotangent.astype(jnp.float32) - to_top
    top_adjoint = solve_level(top_accum.astype(jnp.bfloat16), top_inverse).astype(jnp.bfloat16)
    leaf_rows = pick_rows(
        parent_ext, mid_near_ids, own_leaf_parents, own_leaf_codes, 0
    ) + pick_rows(grand_ext, top_far_ids, own_leaf_grand, own_leaf_codes, NB)
    leaf_rows = mask_columns(leaf_rows.astype(jnp.bfloat16), leaf_valid)
    mid_rows = pick_rows(grand_ext, top_far_ids, own_mid_parents, own_mid_codes, 0)
    mid_rows = mask_columns(mid_rows.astype(jnp.bfloat16), mid_valid)
    leaf_probes = lax.all_gather(leaf_adjoint, "rhs", axis=1, tiled=True)
    leaf_cols = lax.all_to_all(leaf_rows, "rhs", split_axis=2, concat_axis=1, tiled=True)
    leaf_grad = tile_grad(leaf_cols, leaf_probes)
    mid_probes = lax.all_gather(mid_adjoint, "rhs", axis=1, tiled=True)
    mid_cols = lax.all_to_all(mid_rows, "rhs", split_axis=2, concat_axis=1, tiled=True)
    mid_grad = tile_grad(mid_cols, mid_probes)
    return (
        leaf_adjoint,
        mid_adjoint,
        top_adjoint,
        leaf_grad.astype(jnp.bfloat16),
        mid_grad.astype(jnp.bfloat16),
    )


def solution(mesh):
    placed = (
        P(),
        P(),
        P(),
        P(),
        P("leaf"),
        P("leaf"),
        P("leaf", None, None),
        P("leaf", None, None),
        P("leaf", None, None),
        P("leaf", None, None),
        P("leaf", None, None),
        P("leaf", "rhs", None),
        P("leaf", "rhs", None),
        P("leaf", "rhs", None),
        P("leaf", "rhs", None),
        P("leaf", "rhs", None),
    )
    return jax.shard_map(
        shards,
        mesh=mesh,
        in_specs=placed,
        out_specs=(
            P("leaf", "rhs", None),
            P("leaf", "rhs", None),
            P("leaf", "rhs", None),
            P("leaf", "rhs", None),
            P("leaf", "rhs", None),
        ),
        check_vma=False,
    )
```

profile of v0, /device:TPU:0, one launch (start us, length us, event | category | flops | bytes accessed | tf_op | source)
XLA Modules:
  0.0 89.1 jit_solution(4280837738562392103)
XLA Ops:
  0.7 1.4 %collective-permute-start.8 = (bf16[1,32,512]{2,1,0:T(8,128)(2,1)}, bf16[1,32,512]{2,1,0:T(8,128)(2,1)S(1)}, u32[]{:S(2)}, u32[]{:S(2)}) collective-permute-start(bf16[1,32,512]{2,1,0:T(8,128)(2,1)} %param.31), channel_id=1, source_target_pairs={{4,0},{8,4},{12,8},{16,12},{20,16},{24,20},{28,24},{5,1},{9,5},{13... | collective-permute-start | bytes 98312 | tf_op jit(solution)/shard_map/ppermute | solution.py:27
  2.1 5.5 %collective-permute-start.7 = (bf16[1,32,512]{2,1,0:T(8,128)(2,1)}, bf16[1,32,512]{2,1,0:T(8,128)(2,1)S(1)}, u32[]{:S(2)}, u32[]{:S(2)}) collective-permute-start(bf16[1,32,512]{2,1,0:T(8,128)(2,1)} %param.31), channel_id=1, source_target_pairs={{0,4},{4,8},{8,12},{12,16},{16,20},{20,24},{24,28},{1,5},{5,9},{9,... | collective-permute-start | bytes 98312 | tf_op jit(solution)/shard_map/ppermute | solution.py:27
  7.6 4.0 %collective-permute-start.6 = (bf16[1,32,512]{2,1,0:T(8,128)(2,1)}, bf16[1,32,512]{2,1,0:T(8,128)(2,1)S(1)}, u32[]{:S(2)}, u32[]{:S(2)}) collective-permute-start(bf16[1,32,512]{2,1,0:T(8,128)(2,1)} %param.31), channel_id=1, source_target_pairs={{0,8},{4,12},{8,16},{12,20},{16,24},{20,28},{1,9},{5,13},{9,17},{1... | collective-permute-start | bytes 98312 | tf_op jit(solution)/shard_map/ppermute | solution.py:27
  11.6 1.3 %collective-permute-start.9 = (bf16[1,32,512]{2,1,0:T(8,128)(2,1)}, bf16[1,32,512]{2,1,0:T(8,128)(2,1)S(1)}, u32[]{:S(2)}, u32[]{:S(2)}) collective-permute-start(bf16[1,32,512]{2,1,0:T(8,128)(2,1)} %param.31), channel_id=1, source_target_pairs={{8,0},{12,4},{16,8},{20,12},{24,16},{28,20},{9,1},{13,5},{17,9},{2... | collective-permute-start | bytes 98312 | tf_op jit(solution)/shard_map/ppermute | solution.py:27
  12.9 5.0 %collective-permute-start.4 = (bf16[2,32,512]{2,1,0:T(8,128)(2,1)}, bf16[2,32,512]{2,1,0:T(8,128)(2,1)}, u32[]{:S(2)}, u32[]{:S(2)}) collective-permute-start(bf16[2,32,512]{2,1,0:T(8,128)(2,1)} %param.30), channel_id=1, source_target_pairs={{0,4},{4,8},{8,12},{12,16},{16,20},{20,24},{24,28},{1,5},{5,9},{9,... | collective-permute-start | bytes 196616 | tf_op jit(solution)/shard_map/ppermute | solution.py:16
  19.6 0.8 select_reduce_fusion.2
  20.5 0.8 select_reduce_fusion.1
  21.3 0.8 select_reduce_fusion
  25.3 0.9 %fusion.45 = s32[6]{0:T(128)S(1)} fusion(s32[6]{0:T(128)S(1)} %iota_add_fusion.1, s32[16]{0:T(128)} %bitcast.143), kind=kLoop, calls=%fused_computation.78 | loop fusion | flops 282 | bytes 112 | tf_op jit(solution)/shard_map/reduce_sum | solution.py:61
  28.0 1.0 %fusion.33 = s32[12]{0:T(128)S(1)} fusion(s32[12]{0:T(128)S(1)} %iota_add_fusion.3, s32[32]{0:T(128)} %bitcast.142), kind=kLoop, calls=%fused_computation.64 | loop fusion | flops 1140 | bytes 224 | tf_op jit(solution)/shard_map/reduce_sum | solution.py:61
  30.0 1.6 %convolution_convert_fusion = bf16[4,32,512]{2,1,0:T(8,128)(2,1)S(1)} fusion(bf16[4,32,512]{2,1,0:T(8,128)(2,1)} %param.27, bf16[4,512,512]{2,1,0:T(8,128)(2,1)S(1)} %copy-done), kind=kOutput, calls=%fused_computation.2 | convolution fusion | flops 67174400 | bytes 2359296 | tf_op jit(solution)/shard_map/dot_general | solution.py:31
  31.9 7.3 %all_gather.6 = bf16[4,128,512]{2,1,0:T(8,128)(2,1)S(1)} all-gather(bf16[4,32,512]{2,1,0:T(8,128)(2,1)S(1)} %convolution_convert_fusion), channel_id=1, replica_groups=mesh['leaf'=8,'rhs'=4] {'rhs'}, dimensions={1}, use_global_device_ids=true | all-gather | bytes 655360 | tf_op jit(solution)/shard_map/all_gather | solution.py:164
  39.2 1.3 %collective-permute-start.5 = (bf16[2,32,512]{2,1,0:T(8,128)(2,1)}, bf16[2,32,512]{2,1,0:T(8,128)(2,1)}, u32[]{:S(2)}, u32[]{:S(2)}) collective-permute-start(bf16[2,32,512]{2,1,0:T(8,128)(2,1)} %param.30), channel_id=1, source_target_pairs={{4,0},{8,4},{12,8},{16,12},{20,16},{24,20},{28,24},{5,1},{9,5},{13... | collective-permute-start | bytes 196616 | tf_op jit(solution)/shard_map/ppermute | solution.py:19
  40.6 1.3 %collective-permute-start.1 = (f32[4,32,128]{2,1,0:T(8,128)S(1)}, f32[4,32,128]{2,1,0:T(8,128)S(1)}, u32[]{:S(2)}, u32[]{:S(2)}) collective-permute-start(f32[4,32,128]{2,1,0:T(8,128)S(1)} %convolution_select_fusion), channel_id=1, source_target_pairs={{4,0},{8,4},{12,8},{16,12},{20,16},{24,20},{28,24},{5,1},{9,5},{13... | collective-permute-start | bytes 196616 | tf_op jit(solution)/shard_map/ppermute | solution.py:19
  41.9 5.2 %collective-permute-start = (f32[4,32,128]{2,1,0:T(8,128)S(1)}, f32[4,32,128]{2,1,0:T(8,128)S(1)}, u32[]{:S(2)}, u32[]{:S(2)}) collective-permute-start(f32[4,32,128]{2,1,0:T(8,128)S(1)} %convolution_select_fusion), channel_id=1, source_target_pairs={{0,4},{4,8},{8,12},{12,16},{16,20},{20,24},{24,28},{1,5},{5,9},{9,... | collective-permute-start | bytes 196616 | tf_op jit(solution)/shard_map/ppermute | solution.py:16
  48.4 3.3 %all-to-all-start.1 = ((bf16[4,2,1024]{2,1,0:T(2,128)(2,1)}), bf16[4,2,1024]{2,1,0:T(2,128)(2,1)S(1)}, u32[]{:S(2)}, u32[]{:S(2)}) async-start(bf16[4,2,1024]{2,1,0:T(2,128)(2,1)} %reshape.647), calls=%async_computation.1 | async-start | bytes 32768 | tf_op jit(solution)/shard_map/all_to_all | solution.py:168
  51.6 0.9 %convolution_bitcast_fusion.2 = f32[32,128,4]{1,2,0:T(4,128)} fusion(bf16[5,32,4,128]{3,2,1,0:T(4,128)(2,1)S(1)} %reshape.631, pred[4,4]{1,0:T(4,128)(4,1)S(1)} %get-tuple-element.12, pred[4,5]{0,1:T(8,128)(4,1)S(1)} %broadcast_compare_fusion.1), kind=kOutput, calls=%fused_computation.8 | convolution fusion | flops 655440 | bytes 229412 | tf_op jit(solution)/shard_map/smeb,enbc->snmc/dot_general | solution.py:90
  52.5 2.9 %all-to-all-done.1 = bf16[4,2,1024]{2,1,0:T(2,128)(2,1)S(1)} async-done(((bf16[4,2,1024]{2,1,0:T(2,128)(2,1)}), bf16[4,2,1024]{2,1,0:T(2,128)(2,1)S(1)}, u32[]{:S(2)}, u32[]{:S(2)}) %all-to-all-start.1) | async-done | bytes 16416 | tf_op jit(solution)/shard_map/all_to_all | solution.py:168
  56.9 1.6 %convolution_convert_fusion.1 = bf16[2,32,512]{2,1,0:T(8,128)(2,1)S(1)} fusion(bf16[2,512,512]{2,1,0:T(8,128)(2,1)} %param.23, f32[2,32,512]{2,0,1:T(2,128)S(1)} %reshape.625, bf16[2,32,512]{2,1,0:T(8,128)(2,1)S(1)} %copy-done.6), kind=kOutput, calls=%fused_computation.6 | convolution fusion | flops 33685504 | bytes 1310720 | tf_op jit(solution)/shard_map/dot_general | solution.py:31
  60.1 1.3 %collective-permute-start.3 = (f32[2,32,640]{2,0,1:T(2,128)}, f32[2,32,640]{2,0,1:T(2,128)}, u32[]{:S(2)}, u32[]{:S(2)}) collective-permute-start(f32[2,32,640]{2,0,1:T(2,128)} %constant_dynamic-update-slice_fusion), channel_id=1, source_target_pairs={{4,0},{8,4},{12,8},{16,12},{20,16},{24,20},{28,24},{5,1},{9,5},{13... | collective-permute-start | bytes 491528 | tf_op jit(solution)/shard_map/ppermute | solution.py:19
  61.4 6.1 %collective-permute-start.2 = (f32[2,32,640]{2,0,1:T(2,128)}, f32[2,32,640]{2,0,1:T(2,128)}, u32[]{:S(2)}, u32[]{:S(2)}) collective-permute-start(f32[2,32,640]{2,0,1:T(2,128)} %constant_dynamic-update-slice_fusion), channel_id=1, source_target_pairs={{0,4},{4,8},{8,12},{12,16},{16,20},{20,24},{24,28},{1,5},{5,9},{9,... | collective-permute-start | bytes 491528 | tf_op jit(solution)/shard_map/ppermute | solution.py:16
  67.5 5.8 %all_gather.7 = bf16[2,128,512]{2,1,0:T(8,128)(2,1)S(1)} all-gather(bf16[2,32,512]{2,1,0:T(8,128)(2,1)S(1)} %convolution_convert_fusion.1), channel_id=1, replica_groups=mesh['leaf'=8,'rhs'=4] {'rhs'}, dimensions={1}, use_global_device_ids=true | all-gather | bytes 327680 | tf_op jit(solution)/shard_map/all_gather | solution.py:167
  73.3 0.9 %pad_maximum_fusion.4 = bf16[6,32,512]{2,1,0:T(8,128)(2,1)S(1)} fusion(bf16[2,32,512]{2,1,0:T(8,128)(2,1)} %collective-permute-done.5, bf16[2,32,512]{2,1,0:T(8,128)(2,1)} %param.30, bf16[2,32,512]{2,1,0:T(8,128)(2,1)} %collective-permute-done.4), kind=kLoop, calls=%fused_computation.23 | loop fusion | flops 196608 | bytes 393216 | tf_op jit(solution)/shard_map/concatenate | solution.py:20
  74.3 1.0 %convolution_bitcast_fusion.3 = f32[32,128,4]{1,2,0:T(4,128)S(1)} fusion(bf16[6,32,4,128]{3,2,1,0:T(4,128)(2,1)S(1)} %reshape.630, pred[4,4]{1,0:T(4,128)(4,1)} %get-tuple-element.13, pred[4,6]{0,1:T(8,128)(4,1)} %broadcast_compare_fusion.2), kind=kOutput, calls=%fused_computation.9 | convolution fusion | flops 786528 | bytes 262184 | tf_op jit(solution)/shard_map/smeb,enbc->snmc/dot_general | solution.py:90
  75.2 0.9 fusion.21
  77.0 3.4 %all-to-all-start = ((bf16[4,2,2048]{2,1,0:T(2,128)(2,1)}), bf16[4,2,2048]{2,1,0:T(2,128)(2,1)S(1)}, u32[]{:S(2)}, u32[]{:S(2)}) async-start(bf16[4,2,2048]{2,1,0:T(2,128)(2,1)} %reshape.645), calls=%async_computation | async-start | bytes 65536 | tf_op jit(solution)/shard_map/all_to_all | solution.py:165
  80.4 0.8 fusion.1
  81.2 3.1 %all-to-all-done = bf16[4,2,2048]{2,1,0:T(2,128)(2,1)S(1)} async-done(((bf16[4,2,2048]{2,1,0:T(2,128)(2,1)}), bf16[4,2,2048]{2,1,0:T(2,128)(2,1)S(1)}, u32[]{:S(2)}, u32[]{:S(2)}) %all-to-all-start) | async-done | bytes 32800 | tf_op jit(solution)/shard_map/all_to_all | solution.py:165
  84.7 0.9 fusion
  85.6 1.6 %fusion.3 = f32[1,32,512]{2,0,1:T(1,128)S(1)} fusion(f32[2,32,640]{2,0,1:T(2,128)} %collective-permute-done.3, f32[2,32,640]{2,0,1:T(2,128)} %constant_dynamic-update-slice_fusion, f32[2,32,640]{2,0,1:T(2,128)} %collective-permute-done.2, pred[6]{0:T(512)(128)(4,1)} %select_compare_fusion), kind=kOutput, calls=%fused_computation.16 | convolution fusion | flops 1376256 | bytes 557062 | tf_op jit(solution)/shard_map/te,enw->tnw/dot_general | solution.py:153
  87.2 1.0 %fusion.8 = f32[32,128,4]{1,2,0:T(4,128)S(1)} fusion(f32[2,32,640]{2,0,1:T(2,128)} %collective-permute-done.3, f32[2,32,640]{2,0,1:T(2,128)} %constant_dynamic-update-slice_fusion, f32[2,32,640]{2,0,1:T(2,128)} %collective-permute-done.2, s32[6]{0:T(128)} %broadcast_select_fusion.1, pred[6]{0:T(512)(128)(4,1)} %select_compare_fusion), kind=kOutput, calls=%fused_computation.24 | convolution fusion | flops 1228848 | bytes 557086 | tf_op jit(solution)/shard_map/temb,enmc->tnbc/dot_general | solution.py:77
  88.2 0.9 fusion.2
  (86 shorter events, 13.4 us)
Async XLA Ops:
  0.6 29.4 %copy-start = (bf16[4,512,512]{2,1,0:T(8,128)(2,1)S(1)}, bf16[4,512,512]{2,1,0:T(8,128)(2,1)}, u32[]{:S(2)}) copy-start(bf16[4,512,512]{2,1,0:T(8,128)(2,1)} %param.22) | copy-start | bytes 6291460
  0.6 41.2 %copy-start.8 = (bf16[1,32,512]{2,1,0:T(8,128)(2,1)S(1)}, bf16[1,32,512]{2,1,0:T(8,128)(2,1)}, u32[]{:S(2)}) copy-start(bf16[1,32,512]{2,1,0:T(8,128)(2,1)} %param.31) | copy-start | bytes 98308
  0.7 31.0 %copy-start.3 = (bf16[4,128,512]{2,1,0:T(8,128)(2,1)S(1)}, bf16[4,128,512]{2,1,0:T(8,128)(2,1)}, u32[]{:S(2)}) copy-start(bf16[4,128,512]{2,1,0:T(8,128)(2,1)} %param.25) | copy-start | bytes 1572868
  0.7 41.2 %collective-permute-start.8 = (bf16[1,32,512]{2,1,0:T(8,128)(2,1)}, bf16[1,32,512]{2,1,0:T(8,128)(2,1)S(1)}, u32[]{:S(2)}, u32[]{:S(2)}) collective-permute-start(bf16[1,32,512]{2,1,0:T(8,128)(2,1)} %param.31), channel_id=1, source_target_pairs={{4,0},{8,4},{12,8},{16,12},{20,16},{24,20},{28,24},{5,1},{9,5},{13... | collective-permute-start | bytes 98312 | tf_op jit(solution)/shard_map/ppermute | solution.py:27
  2.1 38.5 %collective-permute-start.7 = (bf16[1,32,512]{2,1,0:T(8,128)(2,1)}, bf16[1,32,512]{2,1,0:T(8,128)(2,1)S(1)}, u32[]{:S(2)}, u32[]{:S(2)}) collective-permute-start(bf16[1,32,512]{2,1,0:T(8,128)(2,1)} %param.31), channel_id=1, source_target_pairs={{0,4},{4,8},{8,12},{12,16},{16,20},{20,24},{24,28},{1,5},{5,9},{9,... | collective-permute-start | bytes 98312 | tf_op jit(solution)/shard_map/ppermute | solution.py:27
  7.6 31.6 %collective-permute-start.6 = (bf16[1,32,512]{2,1,0:T(8,128)(2,1)}, bf16[1,32,512]{2,1,0:T(8,128)(2,1)S(1)}, u32[]{:S(2)}, u32[]{:S(2)}) collective-permute-start(bf16[1,32,512]{2,1,0:T(8,128)(2,1)} %param.31), channel_id=1, source_target_pairs={{0,8},{4,12},{8,16},{12,20},{16,24},{20,28},{1,9},{5,13},{9,17},{1... | collective-permute-start | bytes 98312 | tf_op jit(solution)/shard_map/ppermute | solution.py:27
  11.6 35.5 %collective-permute-start.9 = (bf16[1,32,512]{2,1,0:T(8,128)(2,1)}, bf16[1,32,512]{2,1,0:T(8,128)(2,1)S(1)}, u32[]{:S(2)}, u32[]{:S(2)}) collective-permute-start(bf16[1,32,512]{2,1,0:T(8,128)(2,1)} %param.31), channel_id=1, source_target_pairs={{8,0},{12,4},{16,8},{20,12},{24,16},{28,20},{9,1},{13,5},{17,9},{2... | collective-permute-start | bytes 98312 | tf_op jit(solution)/shard_map/ppermute | solution.py:27
  12.9 60.3 %collective-permute-start.4 = (bf16[2,32,512]{2,1,0:T(8,128)(2,1)}, bf16[2,32,512]{2,1,0:T(8,128)(2,1)}, u32[]{:S(2)}, u32[]{:S(2)}) collective-permute-start(bf16[2,32,512]{2,1,0:T(8,128)(2,1)} %param.30), channel_id=1, source_target_pairs={{0,4},{4,8},{8,12},{12,16},{16,20},{20,24},{24,28},{1,5},{5,9},{9,... | collective-permute-start | bytes 196616 | tf_op jit(solution)/shard_map/ppermute | solution.py:16
  23.1 8.6 %copy-start.9 = (pred[4,128]{1,0:T(4,128)(4,1)}, pred[4,128]{1,0:T(4,128)(4,1)S(1)}, u32[]{:S(2)}) copy-start(pred[4,128]{1,0:T(4,128)(4,1)S(1)} %iota_compare_fusion.8) | copy-start | bytes 1540
  23.8 23.7 %copy-start.10 = (pred[2,128]{1,0:T(4,128)(4,1)}, pred[2,128]{1,0:T(4,128)(4,1)S(1)}, u32[]{:S(2)}) copy-start(pred[2,128]{1,0:T(4,128)(4,1)S(1)} %iota_compare_fusion.10) | copy-start | bytes 772
  31.7 25.0 %copy-start.1 = (bf16[4,32,512]{2,1,0:T(8,128)(2,1)}, bf16[4,32,512]{2,1,0:T(8,128)(2,1)S(1)}, u32[]{:S(2)}) copy-start(bf16[4,32,512]{2,1,0:T(8,128)(2,1)S(1)} %convolution_convert_fusion) | copy-start | bytes 393220
  31.9 24.9 %copy-start.6 = (bf16[2,32,512]{2,1,0:T(8,128)(2,1)S(1)}, bf16[2,32,512]{2,1,0:T(8,128)(2,1)}, u32[]{:S(2)}) copy-start(bf16[2,32,512]{2,1,0:T(8,128)(2,1)} %param.28) | copy-start | bytes 196612
  39.2 34.0 %collective-permute-start.5 = (bf16[2,32,512]{2,1,0:T(8,128)(2,1)}, bf16[2,32,512]{2,1,0:T(8,128)(2,1)}, u32[]{:S(2)}, u32[]{:S(2)}) collective-permute-start(bf16[2,32,512]{2,1,0:T(8,128)(2,1)} %param.30), channel_id=1, source_target_pairs={{4,0},{8,4},{12,8},{16,12},{20,16},{24,20},{28,24},{5,1},{9,5},{13... | collective-permute-start | bytes 196616 | tf_op jit(solution)/shard_map/ppermute | solution.py:19
  40.6 15.2 %collective-permute-start.1 = (f32[4,32,128]{2,1,0:T(8,128)S(1)}, f32[4,32,128]{2,1,0:T(8,128)S(1)}, u32[]{:S(2)}, u32[]{:S(2)}) collective-permute-start(f32[4,32,128]{2,1,0:T(8,128)S(1)} %convolution_select_fusion), channel_id=1, source_target_pairs={{4,0},{8,4},{12,8},{16,12},{20,16},{24,20},{28,24},{5,1},{9,5},{13... | collective-permute-start | bytes 196616 | tf_op jit(solution)/shard_map/ppermute | solution.py:19
  41.9 13.8 %collective-permute-start = (f32[4,32,128]{2,1,0:T(8,128)S(1)}, f32[4,32,128]{2,1,0:T(8,128)S(1)}, u32[]{:S(2)}, u32[]{:S(2)}) collective-permute-start(f32[4,32,128]{2,1,0:T(8,128)S(1)} %convolution_select_fusion), channel_id=1, source_target_pairs={{0,4},{4,8},{8,12},{12,16},{16,20},{20,24},{24,28},{1,5},{5,9},{9,... | collective-permute-start | bytes 196616 | tf_op jit(solution)/shard_map/ppermute | solution.py:16
  47.2 11.3 %copy-start.5 = (bf16[2,128,512]{2,1,0:T(8,128)(2,1)S(1)}, bf16[2,128,512]{2,1,0:T(8,128)(2,1)}, u32[]{:S(2)}) copy-start(bf16[2,128,512]{2,1,0:T(8,128)(2,1)} %param.26) | copy-start | bytes 786436
  48.4 7.1 %all-to-all-start.1 = ((bf16[4,2,1024]{2,1,0:T(2,128)(2,1)}), bf16[4,2,1024]{2,1,0:T(2,128)(2,1)S(1)}, u32[]{:S(2)}, u32[]{:S(2)}) async-start(bf16[4,2,1024]{2,1,0:T(2,128)(2,1)} %reshape.647), calls=%async_computation.1 | async-start | bytes 32768 | tf_op jit(solution)/shard_map/all_to_all | solution.py:168
  55.8 2.8 %copy-start.11 = (pred[2,128]{1,0:T(4,128)(4,1)S(1)}, pred[2,128]{1,0:T(4,128)(4,1)}, u32[]{:S(2)}) copy-start(pred[2,128]{1,0:T(4,128)(4,1)} %copy-done.10) | copy-start | bytes 772
  58.5 27.1 %copy-start.2 = (bf16[2,32,512]{2,1,0:T(8,128)(2,1)}, bf16[2,32,512]{2,1,0:T(8,128)(2,1)S(1)}, u32[]{:S(2)}) copy-start(bf16[2,32,512]{2,1,0:T(8,128)(2,1)S(1)} %convolution_convert_fusion.1) | copy-start | bytes 196612
  60.1 25.5 %collective-permute-start.3 = (f32[2,32,640]{2,0,1:T(2,128)}, f32[2,32,640]{2,0,1:T(2,128)}, u32[]{:S(2)}, u32[]{:S(2)}) collective-permute-start(f32[2,32,640]{2,0,1:T(2,128)} %constant_dynamic-update-slice_fusion), channel_id=1, source_target_pairs={{4,0},{8,4},{12,8},{16,12},{20,16},{24,20},{28,24},{5,1},{9,5},{13... | collective-permute-start | bytes 491528 | tf_op jit(solution)/shard_map/ppermute | solution.py:19
  61.4 24.2 %collective-permute-start.2 = (f32[2,32,640]{2,0,1:T(2,128)}, f32[2,32,640]{2,0,1:T(2,128)}, u32[]{:S(2)}, u32[]{:S(2)}) collective-permute-start(f32[2,32,640]{2,0,1:T(2,128)} %constant_dynamic-update-slice_fusion), channel_id=1, source_target_pairs={{0,4},{4,8},{8,12},{12,16},{16,20},{20,24},{24,28},{1,5},{5,9},{9,... | collective-permute-start | bytes 491528 | tf_op jit(solution)/shard_map/ppermute | solution.py:16
  74.2 14.0 %copy-start.7 = (bf16[1,32,512]{2,1,0:T(8,128)(2,1)S(1)}, bf16[1,32,512]{2,1,0:T(8,128)(2,1)}, u32[]{:S(2)}) copy-start(bf16[1,32,512]{2,1,0:T(8,128)(2,1)} %param.29) | copy-start | bytes 98308
  77.0 11.2 %copy-start.4 = (bf16[1,512,512]{2,1,0:T(8,128)(2,1)S(1)}, bf16[1,512,512]{2,1,0:T(8,128)(2,1)}, u32[]{:S(2)}) copy-start(bf16[1,512,512]{2,1,0:T(8,128)(2,1)} %param.24) | copy-start | bytes 1572868
  77.0 7.3 %all-to-all-start = ((bf16[4,2,2048]{2,1,0:T(2,128)(2,1)}), bf16[4,2,2048]{2,1,0:T(2,128)(2,1)S(1)}, u32[]{:S(2)}, u32[]{:S(2)}) async-start(bf16[4,2,2048]{2,1,0:T(2,128)(2,1)} %reshape.645), calls=%async_computation | async-start | bytes 65536 | tf_op jit(solution)/shard_map/all_to_all | solution.py:165
where the time goes:
time: 90.1 us; the launch traced here: 89.1 us
  starting transfers between devices  39 us (43%)
  blocking collectives  13.1 us (15%)
  matrix products  11.8 us (13%)
  other arithmetic  11.7 us (13%)
  local copies, waits for them, and re-layouts  6.33 us (7%)
  waiting for transfers between devices  6.04 us (7%)
  between operations  1.1 us (1%)
    ppermute x3, starting transfers between devices, padded(): lax.ppermute(lax.slice_in_dim(block, block.shape[dim] - width, None, axis...  16.3 us
    ppermute x4, starting transfers between devices, from_behind(): return lax.ppermute(value, axis, pairs)  12.2 us
    all_gather x1, blocking collectives, shards(): leaf_probes = lax.all_gather(leaf_adjoint, 'rhs', axis=1, tiled=True)  7.31 us
    all_gather x1, blocking collectives, shards(): mid_probes = lax.all_gather(mid_adjoint, 'rhs', axis=1, tiled=True)  5.76 us
    reduce_sum x5, other arithmetic, table_pick(): values = jnp.sum(jnp.where(spread_match, table[None], 0), axis=1)  4.45 us
    dot_general x3, matrix products, solve_level(): lax.dot_general(block_rows, inverse, (((2,), (2,)), ((0,), (0,))), prefer...  4.12 us
    ppermute x3, starting transfers between devices, padded(): lax.ppermute(lax.slice_in_dim(block, 0, width, axis=dim), axis, backward)  3.85 us
    all_to_all x1, starting transfers between devices, shards(): lax.all_to_all(leaf_rows, 'rhs', split_axis=2, concat_axis=1, tiled=True)  3.4 us
  transfers between devices with their start and end apart: 12, of which 2 were waited for; matrix products, arithmetic and copies ran while one was open for 29% of the time, Pallas kernels for 0%

commit v1 on v0

--- a/solution.py
+++ b/solution.py
@@ -6,6 +6,19 @@
 BLK = 128
 MR = 128
 NB = 4
+
+
+def gather_around(value, axis, dim):
+    ways = lax.axis_size(axis)
+    up = [(d, (d + 1) % ways) for d in range(ways)]
+    down = [(d, (d - 1) % ways) for d in range(ways)]
+    earlier, later = ([value], [value])
+    for _ in range(ways // 2):
+        earlier.append(lax.ppermute(earlier[-1], axis, up))
+    for _ in range((ways - 1) // 2):
+        later.append(lax.ppermute(later[-1], axis, down))
+    line = jnp.concatenate([*earlier[::-1], *later[1:]], axis=dim)
+    return jnp.roll(line, (lax.axis_index(axis) - ways // 2) * value.shape[dim], axis=dim)
 
 
 def padded(block, sides, width):
@@ -161,7 +174,7 @@
     leaf_rows = mask_columns(leaf_rows.astype(jnp.bfloat16), leaf_valid)
     mid_rows = pick_rows(grand_ext, top_far_ids, own_mid_parents, own_mid_codes, 0)
     mid_rows = mask_columns(mid_rows.astype(jnp.bfloat16), mid_valid)
-    leaf_probes = lax.all_gather(leaf_adjoint, "rhs", axis=1, tiled=True)
+    leaf_probes = gather_around(leaf_adjoint, "rhs", 1)
     leaf_cols = lax.all_to_all(leaf_rows, "rhs", split_axis=2, concat_axis=1, tiled=True)
     leaf_grad = tile_grad(leaf_cols, leaf_probes)
     mid_probes = lax.all_gather(mid_adjoint, "rhs", axis=1, tiled=True)

time: 90.1 us -> 95.4 us (1.059)
  local copies, waits for them, and re-layouts: 6.33 us -> 15.1 us
  blocking collectives: 13.1 us -> 5.89 us
  matrix products: 11.8 us -> 14.1 us
  other arithmetic: 11.7 us -> 12.9 us
    all_gather x1 -> x0, blocking collectives: 7.31 us -> none  [shards(): leaf_probes = lax.all_gather(leaf_adjoint, 'rhs', axis=1, tiled=True)]
    unnamed x33 -> x46, local copies, waits for them, and re-layouts: 2.53 us -> 8.12 us
    ppermute x0 -> x3, waiting for transfers between devices: none -> 1.04 us  [the longest x2 1.04 us: gather_around(): earlier.append(lax.ppermute(earlier[-1], axis, up))]
    dot_general x2, matrix products: 0.43 us -> 1.43 us  [panel_update(): lax.dot_general(adjoint_rows, panel_block, (((2,), (2,)), ((0,), (0,))),...]
  transfers between devices with their start and end apart: 12 -> 15, of which waited for: 2 -> 3; matrix products, arithmetic and copies ran while one was open for 29% -> 40% of each run, Pallas kernels for 0% -> 0%
where the time goes in v1:
time: 95.4 us; the launch traced here: 94.3 us
  starting transfers between devices  39.1 us (41%)
  local copies, waits for them, and re-layouts  15.1 us (16%)
  matrix products  14.1 us (15%)
  other arithmetic  12.9 us (14%)
  waiting for transfers between devices  6.17 us (6%)
  blocking collectives  5.89 us (6%)
  between operations  1.14 us (1%)
    ppermute x3, starting transfers between devices, padded(): lax.ppermute(lax.slice_in_dim(block, block.shape[dim] - width, None, axis...  16.2 us
    ppermute x4, starting transfers between devices, from_behind(): return lax.ppermute(value, axis, pairs)  12.2 us
    unnamed x46, local copies, waits for them, and re-layouts  8.12 us
    all_gather x1, blocking collectives, shards(): mid_probes = lax.all_gather(mid_adjoint, 'rhs', axis=1, tiled=True)  5.89 us
    reduce_sum x5, other arithmetic, table_pick(): values = jnp.sum(jnp.where(spread_match, table[None], 0), axis=1)  4.45 us
    ppermute x3, starting transfers between devices, padded(): lax.ppermute(lax.slice_in_dim(block, 0, width, axis=dim), axis, backward)  4 us
    dot_general x3, matrix products, solve_level(): lax.dot_general(block_rows, inverse, (((2,), (2,)), ((0,), (0,))), prefer...  3.8 us
    all_to_all x1, starting transfers between devices, shards(): lax.all_to_all(leaf_rows, 'rhs', split_axis=2, concat_axis=1, tiled=True)  3.26 us
  transfers between devices with their start and end apart: 15, of which 3 were waited for; matrix products, arithmetic and copies ran while one was open for 40% of the time, Pallas kernels for 0%

profile of v1, /device:TPU:0, one launch (start us, length us, event | category | flops | bytes accessed | tf_op | source)
XLA Modules:
  0.0 94.3 jit_solution(12527298000870740796)
XLA Ops:
  0.7 1.4 %collective-permute-start.8 = (bf16[1,32,512]{2,1,0:T(8,128)(2,1)}, bf16[1,32,512]{2,1,0:T(8,128)(2,1)S(1)}, u32[]{:S(2)}, u32[]{:S(2)}) collective-permute-start(bf16[1,32,512]{2,1,0:T(8,128)(2,1)} %param.31), channel_id=1, source_target_pairs={{4,0},{8,4},{12,8},{16,12},{20,16},{24,20},{28,24},{5,1},{9,5},{13... | collective-permute-start | bytes 98312 | tf_op jit(solution)/shard_map/ppermute | solution.py:40
  2.1 5.5 %collective-permute-start.7 = (bf16[1,32,512]{2,1,0:T(8,128)(2,1)}, bf16[1,32,512]{2,1,0:T(8,128)(2,1)S(1)}, u32[]{:S(2)}, u32[]{:S(2)}) collective-permute-start(bf16[1,32,512]{2,1,0:T(8,128)(2,1)} %param.31), channel_id=1, source_target_pairs={{0,4},{4,8},{8,12},{12,16},{16,20},{20,24},{24,28},{1,5},{5,9},{9,... | collective-permute-start | bytes 98312 | tf_op jit(solution)/shard_map/ppermute | solution.py:40
  7.6 4.0 %collective-permute-start.6 = (bf16[1,32,512]{2,1,0:T(8,128)(2,1)}, bf16[1,32,512]{2,1,0:T(8,128)(2,1)S(1)}, u32[]{:S(2)}, u32[]{:S(2)}) collective-permute-start(bf16[1,32,512]{2,1,0:T(8,128)(2,1)} %param.31), channel_id=1, source_target_pairs={{0,8},{4,12},{8,16},{12,20},{16,24},{20,28},{1,9},{5,13},{9,17},{1... | collective-permute-start | bytes 98312 | tf_op jit(solution)/shard_map/ppermute | solution.py:40
  11.6 1.3 %collective-permute-start.9 = (bf16[1,32,512]{2,1,0:T(8,128)(2,1)}, bf16[1,32,512]{2,1,0:T(8,128)(2,1)S(1)}, u32[]{:S(2)}, u32[]{:S(2)}) collective-permute-start(bf16[1,32,512]{2,1,0:T(8,128)(2,1)} %param.31), channel_id=1, source_target_pairs={{8,0},{12,4},{16,8},{20,12},{24,16},{28,20},{9,1},{13,5},{17,9},{2... | collective-permute-start | bytes 98312 | tf_op jit(solution)/shard_map/ppermute | solution.py:40
  12.9 5.0 %collective-permute-start.4 = (bf16[2,32,512]{2,1,0:T(8,128)(2,1)}, bf16[2,32,512]{2,1,0:T(8,128)(2,1)}, u32[]{:S(2)}, u32[]{:S(2)}) collective-permute-start(bf16[2,32,512]{2,1,0:T(8,128)(2,1)} %param.30), channel_id=1, source_target_pairs={{0,4},{4,8},{8,12},{12,16},{16,20},{20,24},{24,28},{1,5},{5,9},{9,... | collective-permute-start | bytes 196616 | tf_op jit(solution)/shard_map/ppermute | solution.py:29
  25.3 0.9 fusion.46
  28.1 1.0 %fusion.34 = s32[12]{0:T(128)S(1)} fusion(s32[12]{0:T(128)S(1)} %iota_add_fusion.3, s32[32]{0:T(128)} %bitcast.141), kind=kLoop, calls=%fused_computation.73 | loop fusion | flops 1140 | bytes 224 | tf_op jit(solution)/shard_map/reduce_sum | solution.py:74
  30.5 1.6 %convolution_convert_fusion = bf16[4,32,512]{2,1,0:T(8,128)(2,1)S(1)} fusion(bf16[4,32,512]{2,1,0:T(8,128)(2,1)} %param.27, bf16[4,512,512]{2,1,0:T(8,128)(2,1)S(1)} %copy-done), kind=kOutput, calls=%fused_computation.2 | convolution fusion | flops 67174400 | bytes 2359296 | tf_op jit(solution)/shard_map/dot_general | solution.py:44
  32.5 1.3 %collective-permute-start.5 = (bf16[2,32,512]{2,1,0:T(8,128)(2,1)}, bf16[2,32,512]{2,1,0:T(8,128)(2,1)}, u32[]{:S(2)}, u32[]{:S(2)}) collective-permute-start(bf16[2,32,512]{2,1,0:T(8,128)(2,1)} %param.30), channel_id=1, source_target_pairs={{4,0},{8,4},{12,8},{16,12},{20,16},{24,20},{28,24},{5,1},{9,5},{13... | collective-permute-start | bytes 196616 | tf_op jit(solution)/shard_map/ppermute | solution.py:32
  34.5 1.3 %collective-permute-start.1 = (f32[4,32,128]{2,1,0:T(8,128)S(1)}, f32[4,32,128]{2,1,0:T(8,128)}, u32[]{:S(2)}, u32[]{:S(2)}) collective-permute-start(f32[4,32,128]{2,1,0:T(8,128)S(1)} %convolution_select_fusion), channel_id=1, source_target_pairs={{4,0},{8,4},{12,8},{16,12},{20,16},{24,20},{28,24},{5,1},{9,5},{13... | collective-permute-start | bytes 196616 | tf_op jit(solution)/shard_map/ppermute | solution.py:32
  37.0 5.8 %collective-permute-start = (f32[4,32,128]{2,1,0:T(8,128)S(1)}, f32[4,32,128]{2,1,0:T(8,128)}, u32[]{:S(2)}, u32[]{:S(2)}) collective-permute-start(f32[4,32,128]{2,1,0:T(8,128)S(1)} %convolution_select_fusion), channel_id=1, source_target_pairs={{0,4},{4,8},{8,12},{12,16},{16,20},{20,24},{24,28},{1,5},{5,9},{9,... | collective-permute-start | bytes 196616 | tf_op jit(solution)/shard_map/ppermute | solution.py:29
  44.0 1.0 %reshape.631 = bf16[5,32,4,128]{3,2,1,0:T(4,128)(2,1)S(1)} reshape(bf16[5,32,512]{2,1,0:T(8,128)(2,1)} %constant_dynamic-update-slice_fusion.2) | data formatting | bytes 327680 | tf_op jit(solution)/shard_map/reshape | solution.py:102
  46.5 3.3 %all-to-all-start.1 = ((bf16[4,2,1024]{2,1,0:T(2,128)(2,1)}), bf16[4,2,1024]{2,1,0:T(2,128)(2,1)S(1)}, u32[]{:S(2)}, u32[]{:S(2)}) async-start(bf16[4,2,1024]{2,1,0:T(2,128)(2,1)} %reshape.647), calls=%async_computation.1 | async-start | bytes 32768 | tf_op jit(solution)/shard_map/all_to_all | solution.py:181
  49.8 1.8 %convolution_bitcast_fusion.2 = f32[32,128,4]{1,2,0:T(4,128)} fusion(bf16[5,32,4,128]{3,2,1,0:T(4,128)(2,1)} %copy-done.6, pred[4,4]{1,0:T(4,128)(4,1)S(1)} %get-tuple-element.12, pred[4,5]{0,1:T(8,128)(4,1)S(1)} %broadcast_compare_fusion.1), kind=kOutput, calls=%fused_computation.8 | convolution fusion | flops 655440 | bytes 229412 | tf_op jit(solution)/shard_map/smeb,enbc->snmc/dot_general | solution.py:103
  51.6 2.0 %all-to-all-done.1 = bf16[4,2,1024]{2,1,0:T(2,128)(2,1)S(1)} async-done(((bf16[4,2,1024]{2,1,0:T(2,128)(2,1)}), bf16[4,2,1024]{2,1,0:T(2,128)(2,1)S(1)}, u32[]{:S(2)}, u32[]{:S(2)}) %all-to-all-start.1) | async-done | bytes 16416 | tf_op jit(solution)/shard_map/all_to_all | solution.py:181
  55.3 1.1 %convolution_bitcast_fusion.1 = f32[2,32,4,128]{3,2,0,1:T(4,128)S(1)} fusion(f32[12,32,128,1]{2,1,0,3:T(8,128)S(1)} %maximum_bitcast_fusion, pred[12,4]{0,1:T(4,128)(4,1)} %get-tuple-element.11, pred[2,12]{1,0:T(4,128)(4,1)} %copy-done.12), kind=kOutput, calls=%fused_computation.5 | convolution fusion | flops 4718688 | bytes 327752 | tf_op jit(solution)/shard_map/temb,enmc->tnbc/dot_general | solution.py:90
  57.3 1.3 %convolution_convert_fusion.1 = bf16[2,32,512]{2,1,0:T(8,128)(2,1)S(1)} fusion(bf16[2,512,512]{2,1,0:T(8,128)(2,1)S(1)} %copy-done.2, f32[2,32,512]{2,0,1:T(2,128)} %reshape.625, bf16[2,32,512]{2,1,0:T(8,128)(2,1)} %param.28), kind=kOutput, calls=%fused_computation.6 | convolution fusion | flops 33685504 | bytes 1310720 | tf_op jit(solution)/shard_map/dot_general | solution.py:44
  58.6 1.2 %convolution_select_fusion.1 = f32[2,32,128]{2,1,0:T(8,128)S(1)} fusion(bf16[2,32,512]{2,1,0:T(8,128)(2,1)S(1)} %convolution_convert_fusion.1, bf16[2,128,512]{2,1,0:T(8,128)(2,1)} %param.26, pred[2,128]{1,0:T(4,128)(4,1)} %copy-done.11), kind=kOutput, calls=%fused_computation.14 | convolution fusion | flops 8396800 | bytes 360704 | tf_op jit(solution)/shard_map/dot_general | solution.py:57
  61.1 1.4 %collective-permute-start.3 = (f32[2,32,640]{2,0,1:T(2,128)}, f32[2,32,640]{2,0,1:T(2,128)}, u32[]{:S(2)}, u32[]{:S(2)}) collective-permute-start(f32[2,32,640]{2,0,1:T(2,128)} %constant_dynamic-update-slice_fusion), channel_id=1, source_target_pairs={{4,0},{8,4},{12,8},{16,12},{20,16},{24,20},{28,24},{5,1},{9,5},{13... | collective-permute-start | bytes 491528 | tf_op jit(solution)/shard_map/ppermute | solution.py:32
  62.5 5.9 %all_gather.3 = bf16[2,128,512]{2,1,0:T(8,128)(2,1)S(1)} all-gather(bf16[2,32,512]{2,1,0:T(8,128)(2,1)S(1)} %convolution_convert_fusion.1), channel_id=1, replica_groups=mesh['leaf'=8,'rhs'=4] {'rhs'}, dimensions={1}, use_global_device_ids=true | all-gather | bytes 327680 | tf_op jit(solution)/shard_map/all_gather | solution.py:180
  68.4 5.5 %collective-permute-start.2 = (f32[2,32,640]{2,0,1:T(2,128)}, f32[2,32,640]{2,0,1:T(2,128)}, u32[]{:S(2)}, u32[]{:S(2)}) collective-permute-start(f32[2,32,640]{2,0,1:T(2,128)} %constant_dynamic-update-slice_fusion), channel_id=1, source_target_pairs={{0,4},{4,8},{8,12},{12,16},{16,20},{20,24},{24,28},{1,5},{5,9},{9,... | collective-permute-start | bytes 491528 | tf_op jit(solution)/shard_map/ppermute | solution.py:29
  73.9 0.9 pad_maximum_fusion.4
  75.0 1.0 %convolution_bitcast_fusion.3 = f32[32,128,4]{1,2,0:T(4,128)S(1)} fusion(bf16[6,32,4,128]{3,2,1,0:T(4,128)(2,1)S(1)} %reshape.630, pred[4,4]{1,0:T(4,128)(4,1)} %get-tuple-element.13, pred[4,6]{0,1:T(8,128)(4,1)} %broadcast_compare_fusion.2), kind=kOutput, calls=%fused_computation.9 | convolution fusion | flops 786528 | bytes 262184 | tf_op jit(solution)/shard_map/smeb,enbc->snmc/dot_general | solution.py:103
  77.4 3.3 %all-to-all-start = ((bf16[4,2,2048]{2,1,0:T(2,128)(2,1)}), bf16[4,2,2048]{2,1,0:T(2,128)(2,1)S(1)}, u32[]{:S(2)}, u32[]{:S(2)}) async-start(bf16[4,2,2048]{2,1,0:T(2,128)(2,1)} %reshape.645), calls=%async_computation | async-start | bytes 65536 | tf_op jit(solution)/shard_map/all_to_all | solution.py:178
  81.5 3.1 %all-to-all-done = bf16[4,2,2048]{2,1,0:T(2,128)(2,1)S(1)} async-done(((bf16[4,2,2048]{2,1,0:T(2,128)(2,1)}), bf16[4,2,2048]{2,1,0:T(2,128)(2,1)S(1)}, u32[]{:S(2)}, u32[]{:S(2)}) %all-to-all-start) | async-done | bytes 32800 | tf_op jit(solution)/shard_map/all_to_all | solution.py:178
  85.1 1.6 %fusion.3 = f32[1,32,512]{2,0,1:T(1,128)S(1)} fusion(f32[2,32,640]{2,0,1:T(2,128)} %collective-permute-done.3, f32[2,32,640]{2,0,1:T(2,128)} %constant_dynamic-update-slice_fusion, f32[2,32,640]{2,0,1:T(2,128)} %collective-permute-done.2, pred[6]{0:T(512)(128)(4,1)} %select_compare_fusion), kind=kOutput, calls=%fused_computation.16 | convolution fusion | flops 1376256 | bytes 557062 | tf_op jit(solution)/shard_map/te,enw->tnw/dot_general | solution.py:166
  86.7 1.0 %fusion.9 = f32[32,128,4]{1,2,0:T(4,128)S(1)} fusion(f32[2,32,640]{2,0,1:T(2,128)} %collective-permute-done.3, f32[2,32,640]{2,0,1:T(2,128)} %constant_dynamic-update-slice_fusion, f32[2,32,640]{2,0,1:T(2,128)} %collective-permute-done.2, s32[6]{0:T(128)S(1)} %copy-done.14, pred[6]{0:T(512)(128)(4,1)S(1)} %copy-done.13), kind=kOutput, calls=%fused_computation.25 | convolution fusion | flops 1228848 | bytes 557086 | tf_op jit(solution)/shard_map/temb,enmc->tnbc/dot_general | solution.py:90
  88.6 1.0 %collective-permute-done.11 = bf16[4,32,512]{2,1,0:T(8,128)(2,1)S(1)} collective-permute-done((bf16[4,32,512]{2,1,0:T(8,128)(2,1)}, bf16[4,32,512]{2,1,0:T(8,128)(2,1)S(1)}, u32[]{:S(2)}, u32[]{:S(2)}) %collective-permute-start.11) | collective-permute-done | bytes 131104 | tf_op jit(solution)/shard_map/ppermute | solution.py:17
  89.7 0.9 constant_dynamic-update-slice_fusion.13
  90.6 0.9 constant_dynamic-update-slice_fusion.11
  91.6 0.9 constant_dynamic-update-slice_fusion.9
  92.5 0.9 constant_dynamic-update-slice_fusion.7
  (105 shorter events, 24.1 us)
Async XLA Ops:
  0.6 29.9 %copy-start = (bf16[4,512,512]{2,1,0:T(8,128)(2,1)S(1)}, bf16[4,512,512]{2,1,0:T(8,128)(2,1)}, u32[]{:S(2)}) copy-start(bf16[4,512,512]{2,1,0:T(8,128)(2,1)} %param.22) | copy-start | bytes 6291460
  0.6 35.7 %copy-start.9 = (bf16[1,32,512]{2,1,0:T(8,128)(2,1)S(1)}, bf16[1,32,512]{2,1,0:T(8,128)(2,1)}, u32[]{:S(2)}) copy-start(bf16[1,32,512]{2,1,0:T(8,128)(2,1)} %param.31) | copy-start | bytes 98308
  0.7 36.3 %collective-permute-start.8 = (bf16[1,32,512]{2,1,0:T(8,128)(2,1)}, bf16[1,32,512]{2,1,0:T(8,128)(2,1)S(1)}, u32[]{:S(2)}, u32[]{:S(2)}) collective-permute-start(bf16[1,32,512]{2,1,0:T(8,128)(2,1)} %param.31), channel_id=1, source_target_pairs={{4,0},{8,4},{12,8},{16,12},{20,16},{24,20},{28,24},{5,1},{9,5},{13... | collective-permute-start | bytes 98312 | tf_op jit(solution)/shard_map/ppermute | solution.py:40
  2.1 32.4 %collective-permute-start.7 = (bf16[1,32,512]{2,1,0:T(8,128)(2,1)}, bf16[1,32,512]{2,1,0:T(8,128)(2,1)S(1)}, u32[]{:S(2)}, u32[]{:S(2)}) collective-permute-start(bf16[1,32,512]{2,1,0:T(8,128)(2,1)} %param.31), channel_id=1, source_target_pairs={{0,4},{4,8},{8,12},{12,16},{16,20},{20,24},{24,28},{1,5},{5,9},{9,... | collective-permute-start | bytes 98312 | tf_op jit(solution)/shard_map/ppermute | solution.py:40
  7.6 24.9 %collective-permute-start.6 = (bf16[1,32,512]{2,1,0:T(8,128)(2,1)}, bf16[1,32,512]{2,1,0:T(8,128)(2,1)S(1)}, u32[]{:S(2)}, u32[]{:S(2)}) collective-permute-start(bf16[1,32,512]{2,1,0:T(8,128)(2,1)} %param.31), channel_id=1, source_target_pairs={{0,8},{4,12},{8,16},{12,20},{16,24},{20,28},{1,9},{5,13},{9,17},{1... | collective-permute-start | bytes 98312 | tf_op jit(solution)/shard_map/ppermute | solution.py:40
  11.6 31.8 %collective-permute-start.9 = (bf16[1,32,512]{2,1,0:T(8,128)(2,1)}, bf16[1,32,512]{2,1,0:T(8,128)(2,1)S(1)}, u32[]{:S(2)}, u32[]{:S(2)}) collective-permute-start(bf16[1,32,512]{2,1,0:T(8,128)(2,1)} %param.31), channel_id=1, source_target_pairs={{8,0},{12,4},{16,8},{20,12},{24,16},{28,20},{9,1},{13,5},{17,9},{2... | collective-permute-start | bytes 98312 | tf_op jit(solution)/shard_map/ppermute | solution.py:40
  12.9 55.5 %collective-permute-start.4 = (bf16[2,32,512]{2,1,0:T(8,128)(2,1)}, bf16[2,32,512]{2,1,0:T(8,128)(2,1)}, u32[]{:S(2)}, u32[]{:S(2)}) collective-permute-start(bf16[2,32,512]{2,1,0:T(8,128)(2,1)} %param.30), channel_id=1, source_target_pairs={{0,4},{4,8},{8,12},{12,16},{16,20},{20,24},{24,28},{1,5},{5,9},{9,... | collective-permute-start | bytes 196616 | tf_op jit(solution)/shard_map/ppermute | solution.py:29
  23.1 21.9 %copy-start.10 = (pred[4,128]{1,0:T(4,128)(4,1)}, pred[4,128]{1,0:T(4,128)(4,1)S(1)}, u32[]{:S(2)}) copy-start(pred[4,128]{1,0:T(4,128)(4,1)S(1)} %iota_compare_fusion.8) | copy-start | bytes 1540
  23.8 21.9 %copy-start.11 = (pred[2,128]{1,0:T(4,128)(4,1)}, pred[2,128]{1,0:T(4,128)(4,1)S(1)}, u32[]{:S(2)}) copy-start(pred[2,128]{1,0:T(4,128)(4,1)S(1)} %iota_compare_fusion.10) | copy-start | bytes 772
  23.8 8.3 %copy-start.4 = (bf16[4,128,512]{2,1,0:T(8,128)(2,1)S(1)}, bf16[4,128,512]{2,1,0:T(8,128)(2,1)}, u32[]{:S(2)}) copy-start(bf16[4,128,512]{2,1,0:T(8,128)(2,1)} %param.25) | copy-start | bytes 1572868
  29.4 25.5 %copy-start.12 = (pred[2,12]{1,0:T(4,128)(4,1)}, pred[2,12]{1,0:T(4,128)(4,1)S(1)}, u32[]{:S(2)}) copy-start(pred[2,12]{1,0:T(4,128)(4,1)S(1)} %broadcast_compare_fusion.3) | copy-start | bytes 76
  32.2 60.3 %copy-start.1 = (bf16[4,32,512]{2,1,0:T(8,128)(2,1)}, bf16[4,32,512]{2,1,0:T(8,128)(2,1)S(1)}, u32[]{:S(2)}) copy-start(bf16[4,32,512]{2,1,0:T(8,128)(2,1)S(1)} %convolution_convert_fusion) | copy-start | bytes 393220
  32.2 25.1 %copy-start.2 = (bf16[2,512,512]{2,1,0:T(8,128)(2,1)S(1)}, bf16[2,512,512]{2,1,0:T(8,128)(2,1)}, u32[]{:S(2)}) copy-start(bf16[2,512,512]{2,1,0:T(8,128)(2,1)} %param.23) | copy-start | bytes 3145732
  32.5 41.4 %collective-permute-start.5 = (bf16[2,32,512]{2,1,0:T(8,128)(2,1)}, bf16[2,32,512]{2,1,0:T(8,128)(2,1)}, u32[]{:S(2)}, u32[]{:S(2)}) collective-permute-start(bf16[2,32,512]{2,1,0:T(8,128)(2,1)} %param.30), channel_id=1, source_target_pairs={{4,0},{8,4},{12,8},{16,12},{20,16},{24,20},{28,24},{5,1},{9,5},{13... | collective-permute-start | bytes 196616 | tf_op jit(solution)/shard_map/ppermute | solution.py:32
  34.5 19.4 %collective-permute-start.1 = (f32[4,32,128]{2,1,0:T(8,128)S(1)}, f32[4,32,128]{2,1,0:T(8,128)}, u32[]{:S(2)}, u32[]{:S(2)}) collective-permute-start(f32[4,32,128]{2,1,0:T(8,128)S(1)} %convolution_select_fusion), channel_id=1, source_target_pairs={{4,0},{8,4},{12,8},{16,12},{20,16},{24,20},{28,24},{5,1},{9,5},{13... | collective-permute-start | bytes 196616 | tf_op jit(solution)/shard_map/ppermute | solution.py:32
  37.0 17.0 %collective-permute-start = (f32[4,32,128]{2,1,0:T(8,128)S(1)}, f32[4,32,128]{2,1,0:T(8,128)}, u32[]{:S(2)}, u32[]{:S(2)}) collective-permute-start(f32[4,32,128]{2,1,0:T(8,128)S(1)} %convolution_select_fusion), channel_id=1, source_target_pairs={{0,4},{4,8},{8,12},{12,16},{16,20},{20,24},{24,28},{1,5},{5,9},{9,... | collective-permute-start | bytes 196616 | tf_op jit(solution)/shard_map/ppermute | solution.py:29
  43.4 47.2 %collective-permute-start.12 = (bf16[4,32,512]{2,1,0:T(8,128)(2,1)S(1)}, bf16[4,32,512]{2,1,0:T(8,128)(2,1)}, u32[]{:S(2)}, u32[]{:S(2)}) collective-permute-start(bf16[4,32,512]{2,1,0:T(8,128)(2,1)S(1)} %convolution_convert_fusion), channel_id=1, source_target_pairs={{0,3},{1,0},{2,1},{3,2},{4,7},{5,4},{6,5},{7,6},{8,11},{9,8},{10,9... | collective-permute-start | bytes 393224 | tf_op jit(solution)/shard_map/ppermute | solution.py:19
  45.0 0.7 copy-start.6
  46.5 7.1 %all-to-all-start.1 = ((bf16[4,2,1024]{2,1,0:T(2,128)(2,1)}), bf16[4,2,1024]{2,1,0:T(2,128)(2,1)S(1)}, u32[]{:S(2)}, u32[]{:S(2)}) async-start(bf16[4,2,1024]{2,1,0:T(2,128)(2,1)} %reshape.647), calls=%async_computation.1 | async-start | bytes 32768 | tf_op jit(solution)/shard_map/all_to_all | solution.py:181
  53.9 31.1 %collective-permute-start.10 = (bf16[4,32,512]{2,1,0:T(8,128)(2,1)S(1)}, bf16[4,32,512]{2,1,0:T(8,128)(2,1)}, u32[]{:S(2)}, u32[]{:S(2)}) collective-permute-start(bf16[4,32,512]{2,1,0:T(8,128)(2,1)S(1)} %convolution_convert_fusion), channel_id=1, source_target_pairs={{0,1},{1,2},{2,3},{3,0},{4,5},{5,6},{6,7},{7,4},{8,9},{9,10},{10,1... | collective-permute-start | bytes 393224 | tf_op jit(solution)/shard_map/ppermute | solution.py:17
  58.6 28.1 %copy-start.3 = (bf16[2,32,512]{2,1,0:T(8,128)(2,1)}, bf16[2,32,512]{2,1,0:T(8,128)(2,1)S(1)}, u32[]{:S(2)}) copy-start(bf16[2,32,512]{2,1,0:T(8,128)(2,1)S(1)} %convolution_convert_fusion.1) | copy-start | bytes 196612
  58.6 17.3 %copy-start.7 = (f32[32,128,4]{1,2,0:T(4,128)S(1)}, f32[32,128,4]{1,2,0:T(4,128)}, u32[]{:S(2)}) copy-start(f32[32,128,4]{1,2,0:T(4,128)} %convolution_bitcast_fusion.2) | copy-start | bytes 196612
  61.1 26.6 %copy-start.5 = (bf16[1,512,512]{2,1,0:T(8,128)(2,1)S(1)}, bf16[1,512,512]{2,1,0:T(8,128)(2,1)}, u32[]{:S(2)}) copy-start(bf16[1,512,512]{2,1,0:T(8,128)(2,1)} %param.24) | copy-start | bytes 1572868
  61.1 24.0 %collective-permute-start.3 = (f32[2,32,640]{2,0,1:T(2,128)}, f32[2,32,640]{2,0,1:T(2,128)}, u32[]{:S(2)}, u32[]{:S(2)}) collective-permute-start(f32[2,32,640]{2,0,1:T(2,128)} %constant_dynamic-update-slice_fusion), channel_id=1, source_target_pairs={{4,0},{8,4},{12,8},{16,12},{20,16},{24,20},{28,24},{5,1},{9,5},{13... | collective-permute-start | bytes 491528 | tf_op jit(solution)/shard_map/ppermute | solution.py:32
  68.4 16.6 %collective-permute-start.2 = (f32[2,32,640]{2,0,1:T(2,128)}, f32[2,32,640]{2,0,1:T(2,128)}, u32[]{:S(2)}, u32[]{:S(2)}) collective-permute-start(f32[2,32,640]{2,0,1:T(2,128)} %constant_dynamic-update-slice_fusion), channel_id=1, source_target_pairs={{0,4},{4,8},{8,12},{12,16},{16,20},{20,24},{24,28},{1,5},{5,9},{9,... | collective-permute-start | bytes 491528 | tf_op jit(solution)/shard_map/ppermute | solution.py:29
  74.9 11.8 %copy-start.13 = (pred[6]{0:T(512)(128)(4,1)S(1)}, pred[6]{0:T(512)(128)(4,1)}, u32[]{:S(2)}) copy-start(pred[6]{0:T(512)(128)(4,1)} %select_compare_fusion) | copy-start | bytes 22
  74.9 11.8 %copy-start.14 = (s32[6]{0:T(128)S(1)}, s32[6]{0:T(128)}, u32[]{:S(2)}) copy-start(s32[6]{0:T(128)} %broadcast_select_fusion.1) | copy-start | bytes 76
  74.9 12.8 %copy-start.8 = (bf16[1,32,512]{2,1,0:T(8,128)(2,1)S(1)}, bf16[1,32,512]{2,1,0:T(8,128)(2,1)}, u32[]{:S(2)}) copy-start(bf16[1,32,512]{2,1,0:T(8,128)(2,1)} %param.29) | copy-start | bytes 98308
  77.4 7.2 %all-to-all-start = ((bf16[4,2,2048]{2,1,0:T(2,128)(2,1)}), bf16[4,2,2048]{2,1,0:T(2,128)(2,1)S(1)}, u32[]{:S(2)}, u32[]{:S(2)}) async-start(bf16[4,2,2048]{2,1,0:T(2,128)(2,1)} %reshape.645), calls=%async_computation | async-start | bytes 65536 | tf_op jit(solution)/shard_map/all_to_all | solution.py:178
  85.0 4.7 %collective-permute-start.11 = (bf16[4,32,512]{2,1,0:T(8,128)(2,1)}, bf16[4,32,512]{2,1,0:T(8,128)(2,1)S(1)}, u32[]{:S(2)}, u32[]{:S(2)}) collective-permute-start(bf16[4,32,512]{2,1,0:T(8,128)(2,1)} %collective-permute-done.10), channel_id=1, source_target_pairs={{0,1},{1,2},{2,3},{3,0},{4,5},{5,6},{6,7},{7,4},{8,9},{9,10},{10,1... | collective-permute-start | bytes 393224 | tf_op jit(solution)/shard_map/ppermute | solution.py:17
